TPU v7x, 32 devices: a whole 2x2x4 slice. The times are simulated.
32 devices in a mesh: row: 8 (over z, y), col: 4 (over x, core).
Axes of the slice: x: 2, y: 2, z: 4, core: 2. Of those that a mesh axis runs over, the one named last changes fastest.
Arguments:
- layer_input: bfloat16 [1024, 12288], P(None, 'row'), may hold values from -6 to 6
- hidden_pre: bfloat16 [1024, 24576], P(None, 'col'), may hold values from -6 to 6
- out_grad: bfloat16 [1024, 12288], P(None, 'row'), may hold values from -8 to 8
- w_up: bfloat16 [12288, 24576], P('row', 'col'), may hold values from -0.0546875 to 0.0546875
- w_down: bfloat16 [24576, 12288], P('col', 'row'), may hold values from -0.0390625 to 0.0390625
Outputs:
- in_grad: bfloat16 [1024, 12288], P('col', 'row')
- up_grad: bfloat16 [12288, 24576], P('row', 'col')
- down_grad: bfloat16 [24576, 12288], P('col', 'row')
All inputs are finite; a program needn't handle non-finite values.
Results may differ from a plain program's by a relative error of at most 0.0051.
Values may be sent and summed in bfloat16 or wider, within the bound.
A program may use at most 320 MiB of HBM per device.

v0:
```python
import math
import jax
import jax.numpy as jnp
from jax import lax
from jax.sharding import PartitionSpec as P

GELU_COEF = 0.7978845608
CUBIC_COEF = 0.044715
CONTRACT_LAST = (((1,), (1,)), ((), ()))
CONTRACT_FIRST = (((0,), (0,)), ((), ()))


def gelu_value(pre_act):
    inner = GELU_COEF * (pre_act + CUBIC_COEF * pre_act * pre_act * pre_act)
    return 0.5 * pre_act * (1.0 + jnp.tanh(inner))


def gelu_slope(pre_act):
    inner = GELU_COEF * (pre_act + CUBIC_COEF * pre_act * pre_act * pre_act)
    tangent = jnp.tanh(inner)
    return 0.5 * (1.0 + tangent) + 0.5 * pre_act * (1.0 - tangent * tangent) * GELU_COEF * (
        1.0 + 3.0 * CUBIC_COEF * pre_act * pre_act
    )


def body(layer_input, hidden_pre, out_grad, w_up, w_down):
    token_count = out_grad.shape[0]
    scaling = 1.0 / math.sqrt(token_count)
    pre_act = hidden_pre.astype(jnp.float32)
    activated = gelu_value(pre_act).astype(jnp.bfloat16)
    down_total = lax.dot_general(
        activated, out_grad, CONTRACT_FIRST, preferred_element_type=jnp.float32
    )
    down_grad = (down_total * scaling).astype(jnp.bfloat16)
    local_sum = lax.dot_general(out_grad, w_down, CONTRACT_LAST, preferred_element_type=jnp.float32)
    summed = lax.psum(local_sum, "row")
    hidden_grad = (summed * gelu_slope(pre_act)).astype(jnp.bfloat16)
    up_total = lax.dot_general(
        layer_input, hidden_grad, CONTRACT_FIRST, preferred_element_type=jnp.float32
    )
    in_partial = lax.dot_general(
        hidden_grad, w_up, CONTRACT_LAST, preferred_element_type=jnp.float32
    )
    up_grad = (up_total * scaling).astype(jnp.bfloat16)
    in_grad = lax.psum_scatter(in_partial, "col", scatter_dimension=0, tiled=True).astype(
        jnp.bfloat16
    )
    return (in_grad, up_grad, down_grad)


def solution(mesh):
    placed = (P(None, "row"), P(None, "col"), P(None, "row"), P("row", "col"), P("col", "row"))
    return jax.shard_map(
        body,
        mesh=mesh,
        in_specs=placed,
        out_specs=(P("col", "row"), P("row", "col"), P("col", "row")),
        check_vma=False,
    )
```

profile of v0, /device:TPU:0, one launch (start us, length us, event | category | flops | bytes accessed | tf_op | source)
XLA Modules:
  0.0 922.6 jit_solution(7426446463446432995)
XLA Ops:
  7.2 0.0 copy-start
  7.2 0.0 all-reduce.2.cloned.1.call-start
  7.2 1.8 copy-done
  9.1 25.3 %fusion.21 = f32[1024,6144]{1,0:T(8,128)} fusion(bf16[1024,1536]{1,0:T(8,128)(2,1)S(1)} %copy-done, bf16[6144,1536]{1,0:T(8,128)(2,1)} %param.9), kind=kOutput, calls=%fused_computation.29 | convolution fusion | flops 19327352832 | bytes 47185920 | tf_op jit(solution)/shard_map/dot_general | solution.py:35
  34.4 0.0 all-reduce.2.cloned.1.call-update
  34.4 0.0 reduce-scatter.2.cloned.1.call-start
  34.5 745.5 %all-reduce.2.cloned.1.call-done = f32[1024,6144]{1,0:T(8,128)} async-done(((f32[1024,6144]{1,0:T(8,128)}), f32[1024,6144]{1,0:T(8,128)}) %all-reduce.2.cloned.1.call-update) | async-done | bytes 25165840 | tf_op jit(solution)/shard_map/psum | solution.py:36
  780.0 19.7 %fusion.6 = bf16[1024,6144]{1,0:T(8,128)(2,1)S(1)} fusion(f32[1024,6144]{1,0:T(8,128)} %all-reduce.2.cloned.1.call-done, bf16[1024,6144]{1,0:T(8,128)(2,1)} %param.6), kind=kLoop, calls=%fused_computation.15 | loop fusion | flops 125829120 | bytes 50331648 | tf_op jit(solution)/shard_map/convert_element_type | solution.py:37
  799.8 0.0 copy-start.1
  799.8 4.8 copy-done.1
  804.5 24.3 %fusion.22 = f32[1024,1536]{1,0:T(8,128)} fusion(bf16[1024,6144]{1,0:T(8,128)(2,1)S(1)} %fusion.6, bf16[1536,6144]{1,0:T(8,128)(2,1)} %param.8), kind=kOutput, calls=%fused_computation.30 | convolution fusion | flops 19327352832 | bytes 37748736 | tf_op jit(solution)/shard_map/dot_general | solution.py:41
  828.8 0.0 reduce-scatter.2.cloned.1.call-update
  828.9 0.0 copy-start.2
  828.9 31.3 %multiply_convert_fusion = bf16[6144,1536]{1,0:T(8,128)(2,1)} fusion(bf16[1024,1536]{1,0:T(8,128)(2,1)S(1)} %copy-done, bf16[1024,6144]{1,0:T(8,128)(2,1)} %param.6), kind=kOutput, calls=%fused_computation.7 | convolution fusion | flops 19409141760 | bytes 34603008 | tf_op jit(solution)/shard_map/dot_general | solution.py:31
  860.2 0.0 copy-done.2
  860.2 28.7 %fusion.11 = bf16[1536,6144]{0,1:T(8,128)(2,1)} fusion(bf16[1024,6144]{1,0:T(8,128)(2,1)} %copy-done.1, bf16[1024,1536]{1,0:T(8,128)(2,1)S(1)} %copy-done.2), kind=kOutput, calls=%fused_computation.20 | convolution fusion | flops 19346227200 | bytes 34603008 | tf_op jit(solution)/shard_map/dot_general | solution.py:38
  888.8 24.6 %copy.8 = bf16[1536,6144]{1,0:T(8,128)(2,1)} copy(bf16[1536,6144]{0,1:T(8,128)(2,1)} %fusion.11) | data formatting | bytes 37748736
  913.4 0.0 reduce-scatter.2.cloned.1.call-done
  913.4 2.4 convert_element_type.23
Async XLA Ops:
  7.2 1.9 copy-start
  7.2 772.8 %all-reduce.2.cloned.1.call-start = ((), (), s32[]{:S(2)}) async-start(), calls=%async_computation.1 | async-start | bytes 50331648 | tf_op jit(solution)/shard_map/psum | solution.py:36
  34.4 879.0 %reduce-scatter.2.cloned.1.call-start = ((), (), s32[]{:S(2)}) async-start(), calls=%async_computation.2 | async-start | bytes 7864320 | tf_op jit(solution)/shard_map/reduce_scatter | solution.py:45
  799.8 4.8 copy-start.1
  828.9 31.3 %copy-start.2 = (bf16[1024,1536]{1,0:T(8,128)(2,1)S(1)}, bf16[1024,1536]{1,0:T(8,128)(2,1)}, u32[]{:S(2)}) copy-start(bf16[1024,1536]{1,0:T(8,128)(2,1)} %param.5) | copy-start | bytes 9437188
Sparse Core Ops, SparseCore 0:
  34.6 745.4 all-reduce.1
  829.0 57.9 reduce-scatter.1
where the time goes:
time: 923 us
  waiting for transfers between devices  746 us (81%)
  matrix products  110 us (12%)
  local copies, waits for them, and re-layouts  31.2 us (3%)
  other arithmetic  22.1 us (2%)
  between operations  14.1 us (2%)
    psum x1, waiting for transfers between devices, body(): summed = lax.psum(local_sum, 'row')  746 us
    dot_general x1, matrix products, body(): lax.dot_general(activated, out_grad, CONTRACT_FIRST, preferred_element_ty...  31.3 us
    unnamed x7, local copies, waits for them, and re-layouts  31.2 us
    dot_general x1, matrix products, body(): lax.dot_general(layer_input, hidden_grad, CONTRACT_FIRST, preferred_eleme...  28.7 us
    dot_general x1, matrix products, body(): lax.dot_general(out_grad, w_down, CONTRACT_LAST, preferred_element_type=j...  25.3 us
    dot_general x1, matrix products, body(): lax.dot_general(hidden_grad, w_up, CONTRACT_LAST, preferred_element_type=...  24.3 us
    convert_element_type x1, other arithmetic, body(): hidden_grad = (summed * gelu_slope(pre_act)).astype(jnp.bfloat16)  19.7 us
  transfers between devices with their start and end apart: 2, of which 1 were waited for; matrix products, arithmetic and copies ran while one was open for 9% of the time, Pallas kernels for 0%

commit v1 on v0

--- a/solution.py
+++ b/solution.py
@@ -8,6 +8,14 @@
 CUBIC_COEF = 0.044715
 CONTRACT_LAST = (((1,), (1,)), ((), ()))
 CONTRACT_FIRST = (((0,), (0,)), ((), ()))
+
+
+def doubling_sum(shard, name):
+    size, acc = (lax.axis_size(name), shard)
+    for far in [1 << k for k in range(size.bit_length() - 1)]:
+        swap = [(i, i ^ far) for i in range(size)]
+        acc = acc + lax.ppermute(acc, name, swap)
+    return acc
 
 
 def gelu_value(pre_act):
@@ -33,7 +41,7 @@
     )
     down_grad = (down_total * scaling).astype(jnp.bfloat16)
     local_sum = lax.dot_general(out_grad, w_down, CONTRACT_LAST, preferred_element_type=jnp.float32)
-    summed = lax.psum(local_sum, "row")
+    summed = doubling_sum(local_sum, "row")
     hidden_grad = (summed * gelu_slope(pre_act)).astype(jnp.bfloat16)
     up_total = lax.dot_general(
         layer_input, hidden_grad, CONTRACT_FIRST, preferred_element_type=jnp.float32

time: 923 us -> 2380 us (2.58)
  waiting for transfers between devices: 746 us -> 2160 us
  other arithmetic: 22.1 us -> 61.1 us
    ppermute x0 -> x3, waiting for transfers between devices: none -> 2160 us  [doubling_sum(): acc = acc + lax.ppermute(acc, name, swap)]
    psum x1 -> x0, waiting for transfers between devices: 746 us -> none  [body(): summed = lax.psum(local_sum, 'row')]
    add x0 -> x2, other arithmetic: none -> 34.5 us  [doubling_sum(): acc = acc + lax.ppermute(acc, name, swap)]
  transfers between devices with their start and end apart: 2 -> 4, of which waited for: 1 -> 3; matrix products, arithmetic and copies ran while one was open for 9% -> 4% of each run, Pallas kernels for 0% -> 0%
where the time goes in v1:
time: 2380 us
  waiting for transfers between devices  2160 us (91%)
  matrix products  110 us (5%)
  other arithmetic  61.1 us (3%)
  local copies, waits for them, and re-layouts  31.2 us (1%)
    ppermute x3, waiting for transfers between devices, doubling_sum(): acc = acc + lax.ppermute(acc, name, swap)  2160 us
  transfers between devices with their start and end apart: 4, of which 3 were waited for; matrix products, arithmetic and copies ran while one was open for 4% of the time, Pallas kernels for 0%

profile of v1, /device:TPU:0, one launch (start us, length us, event | category | flops | bytes accessed | tf_op | source)
XLA Modules:
  0.0 2381.6 jit_solution(5070269307210259286)
XLA Ops:
  7.2 0.0 copy-start
  7.2 0.0 reduce-scatter.2.cloned.1.call-start
  7.2 1.8 copy-done
  9.1 25.4 %fusion.21 = f32[1024,6144]{1,0:T(8,128)} fusion(bf16[1024,1536]{1,0:T(8,128)(2,1)S(1)} %copy-done, bf16[6144,1536]{1,0:T(8,128)(2,1)} %param.9), kind=kOutput, calls=%fused_computation.29 | convolution fusion | flops 19327352832 | bytes 47185920 | tf_op jit(solution)/shard_map/dot_general | solution.py:43
  34.4 3.0 collective-permute-start
  37.4 540.3 %collective-permute-done = f32[1024,6144]{1,0:T(8,128)} collective-permute-done((f32[1024,6144]{1,0:T(8,128)}, f32[1024,6144]{1,0:T(8,128)}, u32[]{:S(2)}, u32[]{:S(2)}) %collective-permute-start) | collective-permute-done | bytes 25165856 | tf_op jit(solution)/shard_map/ppermute | solution.py:17
  577.7 16.4 add.25
  594.1 1.9 collective-permute-start.1
  596.0 539.4 %collective-permute-done.1 = f32[1024,6144]{1,0:T(8,128)} collective-permute-done((f32[1024,6144]{1,0:T(8,128)S(1)}, f32[1024,6144]{1,0:T(8,128)}, u32[]{:S(2)}, u32[]{:S(2)}) %collective-permute-start.1) | collective-permute-done | bytes 25165856 | tf_op jit(solution)/shard_map/ppermute | solution.py:17
  1135.5 18.1 add.26
  1153.6 2.5 collective-permute-start.2
  1156.1 1078.3 %collective-permute-done.2 = f32[1024,6144]{1,0:T(8,128)} collective-permute-done((f32[1024,6144]{1,0:T(8,128)}, f32[1024,6144]{1,0:T(8,128)}, u32[]{:S(2)}, u32[]{:S(2)}) %collective-permute-start.2) | collective-permute-done | bytes 25165856 | tf_op jit(solution)/shard_map/ppermute | solution.py:17
  2234.4 24.2 %fusion.6 = bf16[1024,6144]{1,0:T(8,128)(2,1)S(1)} fusion(bf16[1024,6144]{1,0:T(8,128)(2,1)} %param.6, f32[1024,6144]{1,0:T(8,128)} %add.26, f32[1024,6144]{1,0:T(8,128)} %collective-permute-done.2), kind=kLoop, calls=%fused_computation.15 | loop fusion | flops 132120576 | bytes 75497472 | tf_op jit(solution)/shard_map/convert_element_type | solution.py:45
  2258.6 0.0 copy-start.1
  2258.6 4.8 copy-done.1
  2263.4 24.3 %fusion.22 = f32[1024,1536]{1,0:T(8,128)} fusion(bf16[1024,6144]{1,0:T(8,128)(2,1)S(1)} %fusion.6, bf16[1536,6144]{1,0:T(8,128)(2,1)} %param.8), kind=kOutput, calls=%fused_computation.30 | convolution fusion | flops 19327352832 | bytes 37748736 | tf_op jit(solution)/shard_map/dot_general | solution.py:49
  2287.7 0.0 reduce-scatter.2.cloned.1.call-update
  2287.7 0.0 copy-start.2
  2287.7 31.4 %multiply_convert_fusion = bf16[6144,1536]{1,0:T(8,128)(2,1)} fusion(bf16[1024,1536]{1,0:T(8,128)(2,1)S(1)} %copy-done, bf16[1024,6144]{1,0:T(8,128)(2,1)} %param.6), kind=kOutput, calls=%fused_computation.7 | convolution fusion | flops 19409141760 | bytes 34603008 | tf_op jit(solution)/shard_map/dot_general | solution.py:39
  2319.1 0.0 copy-done.2
  2319.1 28.7 %fusion.11 = bf16[1536,6144]{0,1:T(8,128)(2,1)} fusion(bf16[1024,6144]{1,0:T(8,128)(2,1)} %copy-done.1, bf16[1024,1536]{1,0:T(8,128)(2,1)S(1)} %copy-done.2), kind=kOutput, calls=%fused_computation.20 | convolution fusion | flops 19346227200 | bytes 34603008 | tf_op jit(solution)/shard_map/dot_general | solution.py:46
  2347.8 24.6 %copy.8 = bf16[1536,6144]{1,0:T(8,128)(2,1)} copy(bf16[1536,6144]{0,1:T(8,128)(2,1)} %fusion.11) | data formatting | bytes 37748736
  2372.4 0.0 reduce-scatter.2.cloned.1.call-done
  2372.4 2.4 convert_element_type.23
Async XLA Ops:
  7.2 1.9 copy-start
  7.2 2365.2 %reduce-scatter.2.cloned.1.call-start = ((), (), s32[]{:S(2)}) async-start(), calls=%async_computation.1 | async-start | bytes 7864320 | tf_op jit(solution)/shard_map/reduce_scatter | solution.py:53
  34.4 543.3 %collective-permute-start = (f32[1024,6144]{1,0:T(8,128)}, f32[1024,6144]{1,0:T(8,128)}, u32[]{:S(2)}, u32[]{:S(2)}) collective-permute-start(f32[1024,6144]{1,0:T(8,128)} %fusion.21), channel_id=1, source_target_pairs={{0,4},{4,0},{8,12},{12,8},{16,20},{20,16},{24,28},{28,24},{1,5},{5... | collective-permute-start | bytes 75497480 | tf_op jit(solution)/shard_map/ppermute | solution.py:17
  594.1 541.3 %collective-permute-start.1 = (f32[1024,6144]{1,0:T(8,128)S(1)}, f32[1024,6144]{1,0:T(8,128)}, u32[]{:S(2)}, u32[]{:S(2)}) collective-permute-start(f32[1024,6144]{1,0:T(8,128)S(1)} %add.25), channel_id=1, source_target_pairs={{0,8},{4,12},{8,0},{12,4},{16,24},{20,28},{24,16},{28,20},{1,9},{5... | collective-permute-start | bytes 75497480 | tf_op jit(solution)/shard_map/ppermute | solution.py:17
  1153.6 1080.8 %collective-permute-start.2 = (f32[1024,6144]{1,0:T(8,128)}, f32[1024,6144]{1,0:T(8,128)}, u32[]{:S(2)}, u32[]{:S(2)}) collective-permute-start(f32[1024,6144]{1,0:T(8,128)} %add.26), channel_id=1, source_target_pairs={{0,16},{4,20},{8,24},{12,28},{16,0},{20,4},{24,8},{28,12},{1,17},{... | collective-permute-start | bytes 75497480 | tf_op jit(solution)/shard_map/ppermute | solution.py:17
  2258.6 4.8 copy-start.1
  2287.7 31.4 %copy-start.2 = (bf16[1024,1536]{1,0:T(8,128)(2,1)S(1)}, bf16[1024,1536]{1,0:T(8,128)(2,1)}, u32[]{:S(2)}) copy-start(bf16[1024,1536]{1,0:T(8,128)(2,1)} %param.5) | copy-start | bytes 9437188
Sparse Core Ops, SparseCore 0:
  2287.8 59.6 reduce-scatter.1
